TPU v7x, 256 devices: a whole 4x4x8 slice. The times are simulated.
256 devices in a mesh: grid: 128 (over z, y, x_hi, core), orb: 2 (over x_lo).
Axes of the slice: x: 4 (x_hi: 2, x_lo: 2; x = x_hi * 2 + x_lo), y: 4, z: 8, core: 2. Of those that a mesh axis runs over, the one named last changes fastest.
Arguments:
- density: float32 [256, 3, 128, 128], P('grid', None, 'orb'), may hold values from -4 to 4
- basis_values: float32 [256, 1280, 768], P(('grid', 'orb')), may hold values from -0.5 to 0.5
- quad_weights: float32 [256, 1280], P(('grid', 'orb')), may hold values from 0.01 to 0.1
- ext_potential: float32 [256, 1280], P(('grid', 'orb')), may hold values from 0 to 4
- batch_blocks: int32 [256, 6], P(('grid', 'orb')), may hold values from 0 to 255, as said below
- domain_blocks: int32 [512, 4], P(('grid', 'orb')), may hold values from 0 to 255, as said below
- coefficients: float32 [512, 4, 128, 128], P(('grid', 'orb')), may hold values from -0.25 to 0.25
Outputs:
- density_out: float32 [256, 3, 128, 128], P('grid', None, 'orb')
- coefficients_out: float32 [512, 4, 128, 128], P(('grid', 'orb'))
Inputs may be any that keep to these rules, and one draw needn't show every extreme that they name: `batch_blocks`: the batches on grid index g (batch numbers g * 256 / 128 onward) list the 6 blocks from (g - 1) * 2 onward, taken modulo 256, each once, in some order. `domain_blocks`: the domains on grid index g list 4 distinct blocks among the 6 blocks from (g - 1) * 2 onward, taken modulo 256, at least one of the first 2 and one of the last 2 of them.
All inputs are finite; a program needn't handle non-finite values.
Results may differ from a plain program's by a relative error of at most 0.0003.
Values sent between devices are 32-bit elements; how exact they have to be, the bound alone decides.
A program may use at most 64 MiB of HBM per device.

v0:
```python
import functools

import jax
import jax.numpy as jnp
from jax import lax
from jax.experimental import pallas as pl
from jax.experimental.pallas import tpu as pltpu
from jax.sharding import PartitionSpec as P

ITERS = 2
STEP_SCALE = 0.5
WIN = 6
F32 = jnp.float32
BF16 = jnp.bfloat16

DIAG = (0, 1, 4, 5, 8, 9)
PAIR_OFF = (2, 6, 10)
CROSS_OFF = (3, 7)
FULL_PAIR = ((0, 1, 2, 3), (6, 7, 8, 9), (12, 13, 14, 15))
FULL_CROSS = ((4, 5), (10, 11))


def split(value):
    high = value.astype(BF16)
    return high, (value - high.astype(F32)).astype(BF16)


def mul(a, b):
    return lax.dot_general(a, b, (((1,), (0,)), ((), ())), preferred_element_type=F32)


def mul_nt(a, b):
    return lax.dot_general(a, b, (((1,), (1,)), ((), ())), preferred_element_type=F32)


def mul3(a, b, product=mul):
    (ah, al), (bh, bl) = a, b
    return product(ah, bh) + (product(ah, bl) + product(al, bh))


def kernel(
    count,
    dens_ref, basis_hbm, quad_ref, ext_ref, batch_ref, domain_ref, coef_ref,
    dens_out, coef_out,
    basis_ref, basis_high, basis_low, scaled_high, scaled_low,
    pair_high, pair_low, cross_high, cross_low,
    coef_now, grad_now, full_win, full_part, full_recv,
    parts, recvs, owns, wins,
    basis_sem, send_sems, recv_sems,
):
    block = coef_ref.shape[2]
    half = block // 2
    points = basis_ref.shape[0]
    domains, listed = coef_ref.shape[:2]
    g = lax.axis_index("grid")
    o = lax.axis_index("orb")
    after = lax.rem(g + 1, count)
    before = lax.rem(g + count - 1, count)
    other = 1 - o
    targets = ((g, other), (after, o), (after, other), (before, o), (before, other))
    mine = pl.ds(pl.multiple_of(o * half, half), half)
    theirs = pl.ds(pl.multiple_of(other * half, half), half)

    fetch = pltpu.make_async_copy(basis_hbm, basis_ref, basis_sem)
    fetch.start()

    barrier = pltpu.get_barrier_semaphore()
    for to_grid, to_orb in targets:
        pl.semaphore_signal(
            barrier, inc=1, device_id=(to_grid, to_orb), device_id_type=pl.DeviceIdType.MESH
        )
    pl.semaphore_wait(barrier, len(targets))

    started = []

    def send(phase, k, source, target):
        copy = pltpu.make_async_remote_copy(
            src_ref=source,
            dst_ref=target,
            send_sem=send_sems.at[phase, k],
            recv_sem=recv_sems.at[phase, k],
            device_id=targets[k],
            device_id_type=pl.DeviceIdType.MESH,
        )
        copy.start()
        started.append(copy)
        return copy

    arriving = [
        send(0, k, dens_ref.at[pl.ds(a, size)], full_win.at[pl.ds(b, size), mine])
        for k, a, size, b in ((3, 0, 5, 11), (4, 0, 5, 11), (1, 1, 5, 0), (2, 1, 5, 0), (0, 0, 6, 5))
    ]
    full_win[5:11, mine] = dens_ref[...]

    total = 2 * count
    anchor = 2 * g - 2

    def position(value):
        return lax.rem(value - anchor + total, total)

    batch_at = [position(batch_ref[0, j]) for j in range(WIN)]
    domain_at = [[position(domain_ref[d, j]) for j in range(listed)] for d in range(domains)]

    def hit(at, w):
        return jnp.maximum(1 - jnp.abs(at - w), 0).astype(F32)

    batch_hits = [[hit(at, w) for at in batch_at] for w in range(WIN)]
    domain_hits = [[[hit(at, w) for at in places] for w in range(WIN)] for places in domain_at]

    def picked(pieces, weights):
        total_of = pieces[0] * weights[0]
        for piece, weight in zip(pieces[1:], weights[1:]):
            total_of = total_of + piece * weight
        return total_of

    masks = [[sum(hits[1:], hits[0]) for hits in by_window] for by_window in domain_hits]
    for d in range(domains):
        for w in range(WIN):
            coef_now[w * block : (w + 1) * block, d * block : (d + 1) * block] = picked(
                [coef_ref[d, j] for j in range(listed)], domain_hits[d][w]
            )

    fetch.wait()
    for w in range(WIN):
        values = picked(
            [basis_ref[:, j * block : (j + 1) * block] for j in range(WIN)], batch_hits[w]
        )
        high, low = split(values.T)
        basis_high[w * block : (w + 1) * block, :] = high
        basis_low[w * block : (w + 1) * block, :] = low

    def rows(w, size=1):
        return slice(w * block, (w + size) * block)

    def set_pair(t, value):
        pair_high[t], pair_low[t] = split(value)

    def set_cross(t, value):
        cross_high[t], cross_low[t] = split(value)

    def joined(aa, ab, ba, bb):
        return jnp.concatenate(
            [jnp.concatenate([aa, ab], axis=1), jnp.concatenate([ba, bb], axis=1)], axis=0
        )

    def density_from_full():
        for t in range(3):
            value = joined(*(full_win[s] for s in FULL_PAIR[t]))
            set_pair(t, 0.5 * (value + value.T))
        for t in range(2):
            upper, lower = FULL_CROSS[t]
            set_cross(t, full_win[upper].T + full_win[lower])

    def load_pairs(win):
        for t in range(3):
            off = win[PAIR_OFF[t]]
            set_pair(t, joined(win[DIAG[2 * t]], off, off.T, win[DIAG[2 * t + 1]]))

    def density_from_window(win):
        load_pairs(win)
        for t in range(2):
            set_cross(t, 2.0 * win[CROSS_OFF[t]].T)

    def potential_step():
        tile = 2 * block

        def step(i, carry):
            lanes = pl.ds(pl.multiple_of(i * tile, tile), tile)
            rho = jnp.zeros((1, tile), F32)
            weighted = []
            for t in range(3):
                high = basis_high[rows(2 * t, 2), lanes]
                twice = high.astype(F32) + 2.0 * basis_low[rows(2 * t, 2), lanes].astype(F32)
                image = mul(pair_high[t], high) + mul(pair_low[t], high)
                rho = rho + jnp.sum(image * twice, axis=0, keepdims=True)
                weighted.append(twice)
            for t in range(2):
                source, sink = rows(2 * t + 1), rows(2 * t + 2)
                high, low = basis_high[source, lanes], basis_low[source, lanes]
                image = mul3((cross_high[t], cross_low[t]), (high, low))
                values = basis_high[sink, lanes].astype(F32) + basis_low[sink, lanes].astype(F32)
                rho = rho + jnp.sum(image * values, axis=0, keepdims=True)
            potential = ext_ref[:, lanes] - jnp.exp(jnp.log(rho * rho + 1.0) * (1.0 / 6.0))
            scale = quad_ref[:, lanes] * potential
            for t in range(3):
                high, low = split(weighted[t] * scale)
                scaled_high[rows(2 * t, 2), lanes] = high
                scaled_low[rows(2 * t, 2), lanes] = low
            return carry

        lax.fori_loop(0, points // tile, step, 0)

    def fock_part(left, right):
        return mul_nt(basis_high[left, :], scaled_high[right, :]) + mul_nt(
            basis_high[left, :], scaled_low[right, :]
        )

    def put_pair(part, t, value):
        part[DIAG[2 * t]] = value[:block, :block]
        part[DIAG[2 * t + 1]] = value[block:, block:]
        part[PAIR_OFF[t]] = value[:block, block:]

    def fock_pair(part, t):
        value = fock_part(rows(2 * t, 2), rows(2 * t, 2))
        put_pair(part, t, 0.5 * (value + value.T))

    def fock_cross(part, t):
        low, high = rows(2 * t + 1), rows(2 * t + 2)
        part[CROSS_OFF[t]] = 0.5 * (fock_part(low, high) + fock_part(high, low).T)

    def outer_pair(values, t):
        high, low = values
        at = rows(2 * t, 2)
        return mul3((high[at], low[at]), (high[at], low[at]), mul_nt)

    def outer_block(values, left, right):
        high, low = values
        left, right = rows(left), rows(right)
        return mul3((high[left], low[left]), (high[right], low[right]), mul_nt)

    def reduce_and_gather(index, make_pair, make_cross):
        part, recv, own, win = parts.at[index], recvs.at[index], owns.at[index], wins.at[index]
        phase = 1 + 2 * index
        make_pair(part, 0)
        make_cross(part, 0)
        coming = {}
        for k, to_rows in ((3, mine), (4, theirs)):
            coming[k] = send(phase, k, part.at[pl.ds(0, 4), to_rows], recv.at[k, pl.ds(0, 4)])
        make_pair(part, 2)
        for k, to_rows in ((1, mine), (2, theirs)):
            coming[k] = send(phase, k, part.at[pl.ds(8, 3), to_rows], recv.at[k, pl.ds(0, 3)])
        make_pair(part, 1)
        make_cross(part, 1)
        coming[0] = send(phase, 0, part.at[pl.ds(4, 4), theirs], recv.at[0, pl.ds(0, 4)])
        for k in range(5):
            coming[k].wait_recv()
        own[0:3] = part[4:7, mine] + ((recv[0, 0:3] + recv[1, 0:3]) + (recv[2, 0:3] + (recv[3, 0:3] + recv[4, 0:3])))
        own[3] = part[7, mine] + (recv[0, 3] + (recv[3, 3] + recv[4, 3]))
        coming = [
            send(phase + 1, k, own.at[pl.ds(0, size)], win.at[pl.ds(b, size), mine])
            for k, size, b in ((3, 3, 8), (4, 3, 8), (1, 4, 0), (2, 4, 0), (0, 4, 4))
        ]
        win[4:8, mine] = own[...]
        for copy in coming:
            copy.wait_recv()
        return win

    def domain_step(win):
        load_pairs(win)
        for t in range(2):
            set_cross(t, win[CROSS_OFF[t]])
        current = coef_now[...]
        now = split(current)
        for t in range(3):
            at = rows(2 * t, 2)
            grad_now[at] = mul3((pair_high[t], pair_low[t]), (now[0][at], now[1][at]))
        for t in range(2):
            low, high = rows(2 * t + 1), rows(2 * t + 2)
            factor = (cross_high[t], cross_low[t])
            grad_now[low] = grad_now[low] + mul3(factor, (now[0][high], now[1][high]))
            turned = split(win[CROSS_OFF[t]].T)
            grad_now[high] = grad_now[high] + mul3(turned, (now[0][low], now[1][low]))
        for d in range(domains):
            lanes = slice(d * block, (d + 1) * block)
            for w in range(WIN):
                grad_now[rows(w), lanes] = grad_now[rows(w), lanes] * masks[d][w]
            grad = grad_now[:, lanes]
            own = current[:, lanes]
            overlap = mul3(split(own.T), split(grad))
            back = mul3((now[0][:, lanes], now[1][:, lanes]), split(overlap))
            coef_now[:, lanes] = own - STEP_SCALE * (grad - back)

    win = None
    for iteration in range(ITERS):
        if iteration == 0:
            for copy in arriving:
                copy.wait_recv()
            density_from_full()
        else:
            density_from_window(win)
        potential_step()
        win = reduce_and_gather(2 * iteration, fock_pair, fock_cross)
        domain_step(win)
        values = split(coef_now[...])
        if iteration + 1 < ITERS:
            win = reduce_and_gather(
                2 * iteration + 1,
                lambda part, t: put_pair(part, t, outer_pair(values, t)),
                lambda part, t: part.__setitem__(CROSS_OFF[t], outer_block(values, 2 * t + 1, 2 * t + 2)),
            )

    def put_full_pair(t):
        value = outer_pair(values, t)
        aa, ab, ba, bb = FULL_PAIR[t]
        full_part[aa] = value[:block, :block]
        full_part[ab] = value[:block, block:]
        full_part[ba] = value[block:, :block]
        full_part[bb] = value[block:, block:]

    def put_full_cross(t):
        upper, lower = FULL_CROSS[t]
        value = outer_block(values, 2 * t + 1, 2 * t + 2)
        full_part[upper] = value
        full_part[lower] = value.T

    phase = send_sems.shape[0] - 1
    coming = {}
    put_full_pair(0)
    put_full_cross(0)
    for k, to_rows in ((3, mine), (4, theirs)):
        coming[k] = send(phase, k, full_part.at[pl.ds(0, 5), to_rows], full_recv.at[k, pl.ds(1, 5)])
    put_full_pair(2)
    put_full_cross(1)
    for k, to_rows in ((1, mine), (2, theirs)):
        coming[k] = send(phase, k, full_part.at[pl.ds(11, 5), to_rows], full_recv.at[k, pl.ds(0, 5)])
    put_full_pair(1)
    coming[0] = send(phase, 0, full_part.at[pl.ds(5, 6), theirs], full_recv.at[0, pl.ds(0, 6)])
    for d in range(domains):
        for j in range(listed):
            coef_out[d, j] = picked(
                [coef_now[rows(w), d * block : (d + 1) * block] for w in range(WIN)],
                [domain_hits[d][w][j] for w in range(WIN)],
            )
    for k in range(5):
        coming[k].wait_recv()
    for s in range(6):
        value = full_part[5 + s, mine] + full_recv[0, s]
        if s < 5:
            value = value + (full_recv[1, s] + full_recv[2, s])
        if s > 0:
            value = value + (full_recv[3, s] + full_recv[4, s])
        dens_out[s] = value
    for copy in started:
        copy.wait_send()


def shards(
    density, basis_values, quad_weights, ext_potential, batch_blocks, domain_blocks, coefficients
):
    own_blocks, offsets, half, block = density.shape
    points, width = basis_values.shape[1:]
    domains, listed = coefficients.shape[:2]
    sums = 2 * ITERS - 1
    vmem = pl.BlockSpec(memory_space=pltpu.VMEM)
    smem = pl.BlockSpec(memory_space=pltpu.SMEM)
    dens, coef = pl.pallas_call(
        functools.partial(kernel, lax.axis_size("grid")),
        out_shape=(
            jax.ShapeDtypeStruct((own_blocks * offsets, half, block), F32),
            jax.ShapeDtypeStruct(coefficients.shape, F32),
        ),
        in_specs=[vmem, pl.BlockSpec(memory_space=pl.ANY), vmem, vmem, smem, smem, vmem],
        out_specs=(vmem, vmem),
        scratch_shapes=[
            pltpu.VMEM((points, width), F32),
            pltpu.VMEM((width, points), BF16),
            pltpu.VMEM((width, points), BF16),
            pltpu.VMEM((width, points), BF16),
            pltpu.VMEM((width, points), BF16),
            pltpu.VMEM((3, 2 * block, 2 * block), BF16),
            pltpu.VMEM((3, 2 * block, 2 * block), BF16),
            pltpu.VMEM((2, block, block), BF16),
            pltpu.VMEM((2, block, block), BF16),
            pltpu.VMEM((width, domains * block), F32),
            pltpu.VMEM((width, domains * block), F32),
            pltpu.VMEM((16, block, block), F32),
            pltpu.VMEM((16, block, block), F32),
            pltpu.VMEM((5, 6, half, block), F32),
            pltpu.VMEM((sums, 11, block, block), F32),
            pltpu.VMEM((sums, 5, 4, half, block), F32),
            pltpu.VMEM((sums, 4, half, block), F32),
            pltpu.VMEM((sums, 11, block, block), F32),
            pltpu.SemaphoreType.DMA,
            pltpu.SemaphoreType.DMA((2 * sums + 2, 5)),
            pltpu.SemaphoreType.DMA((2 * sums + 2, 5)),
        ],
        compiler_params=pltpu.CompilerParams(collective_id=0, has_side_effects=True),
    )(
        density.reshape(own_blocks * offsets, half, block),
        basis_values[0],
        quad_weights,
        ext_potential,
        batch_blocks,
        domain_blocks,
        coefficients,
    )
    return dens.reshape(density.shape), coef


def solution(mesh):
    in_specs = (
        P("grid", None, "orb", None),
        P(("grid", "orb"), None, None),
        P(("grid", "orb"), None),
        P(("grid", "orb"), None),
        P(("grid", "orb"), None),
        P(("grid", "orb"), None),
        P(("grid", "orb"), None, None, None),
    )
    out_specs = (P("grid", None, "orb", None), P(("grid", "orb"), None, None, None))
    return jax.shard_map(shards, mesh=mesh, in_specs=in_specs, out_specs=out_specs, check_vma=False)
```

profile of v0, /device:TPU:33, one launch (start us, length us, event | category | flops | bytes accessed | tf_op | source)
XLA Modules:
  0.0 107.7 jit_solution(13456288884580743848)
XLA Ops:
  0.6 103.6 %shard_map.86 = (f32[6,64,128]{2,1,0:T(8,128)}, f32[2,4,128,128]{3,2,1,0:T(8,128)}) custom-call(f32[6,64,128]{2,1,0:T(8,128)} %bitcast.4, f32[1280,768]{1,0:T(8,128)} %bitcast.3, f32[1,1280]{1,0:T(1,128)} %quad_ref.1, f32[1,1280]{1,0:T(1,128)} %ext_ref.1, s32[1,6]{1,0:T(1,128)} %batch_ref.1, s32[2,4]{1,0:T(2,128)} %domain_ref.1, f32[2,4,128,128]{3,2,1,0:T(8,128)} %coef_ref.1), custom_call_target="tpu_custom_call" | custom-call | tf_op jit(solution)/shard_map/pallas_call | solution.py:346
  104.2 1.6 %copy.11 = f32[2,3,64,128]{3,2,1,0:T(8,128)} copy(f32[2,3,64,128]{3,2,1,0:T(8,128)} %bitcast.5) | data formatting | bytes 393216
  105.8 1.9 %copy.12 = f32[2,4,128,128]{3,2,1,0:T(8,128)} copy(f32[2,4,128,128]{3,2,1,0:T(8,128)} %get-tuple-element.9) | data formatting | bytes 1048576
where the time goes:
time: 108 us
  Pallas kernels  104 us (96%)
  local copies, waits for them, and re-layouts  3.49 us (3%)
    pallas_call x1, Pallas kernels, shards(): pl.pallas_call(functools.partial(kernel, lax.axis_size('grid')), out_shap...  104 us
    unnamed x2, local copies, waits for them, and re-layouts  3.49 us

commit v1 on v0

v1 whole, which is shorter than its diff:
```python
import functools

import jax
import jax.numpy as jnp
from jax import lax
from jax.experimental import pallas as pl
from jax.experimental.pallas import tpu as pltpu
from jax.sharding import PartitionSpec as P

ITERS = 2
STEP_SCALE = 0.5
WIN = 6
F32 = jnp.float32
BF16 = jnp.bfloat16

FULL_CROSS = ((4, 5), (10, 11))


def split(value):
    high = value.astype(BF16)
    return high, (value - high.astype(F32)).astype(BF16)


def mul(a, b):
    return lax.dot_general(a, b, (((1,), (0,)), ((), ())), preferred_element_type=F32)


def mul_nt(a, b):
    return lax.dot_general(a, b, (((1,), (1,)), ((), ())), preferred_element_type=F32)


def mul3(a, b, product=mul):
    (ah, al), (bh, bl) = a, b
    return product(ah, bh) + (product(ah, bl) + product(al, bh))


def kernel(
    count,
    dens_ref, basis_hbm, quad_ref, ext_ref, batch_ref, domain_ref, coef_ref,
    dens_out, coef_out,
    basis_ref, basis_high, basis_low, basis_twice, scaled_high, scaled_low, rho_ref,
    pair_high, pair_low, cross_high, cross_low,
    coef_now, coef_high, coef_low, grad_now,
    full_win, full_part, full_far, full_sib, full_orb,
    parts, far_recvs, sib_recvs, orb_recvs, owns, wins,
    basis_sem, send_sems, recv_sems,
):
    block = coef_ref.shape[2]
    half = block // 2
    points = basis_ref.shape[0]
    domains, listed = coef_ref.shape[:2]
    g = lax.axis_index("grid")
    o = lax.axis_index("orb")
    parity = lax.rem(g, 2)
    sib = g + 1 - 2 * parity
    far = lax.rem(g + count - 1 + 2 * parity, count)
    other = 1 - o
    ORB, SIB, FAR, FAR_CROSS, RELAY = range(5)
    partners = ((g, other), (sib, o), (far, o), (far, other))
    target_of = partners + (partners[SIB],)
    mine = pl.ds(pl.multiple_of(o * half, half), half)
    theirs = pl.ds(pl.multiple_of(other * half, half), half)

    fetch = pltpu.make_async_copy(basis_hbm, basis_ref, basis_sem)
    fetch.start()
    for index in range(parts.shape[0]):
        sib_recvs[index, 3] = jnp.zeros((block, block), F32)
        for k in range(2):
            far_recvs[index, k, 3] = jnp.zeros((half, block), F32)

    barrier = pltpu.get_barrier_semaphore()
    for partner in partners:
        pl.semaphore_signal(
            barrier, inc=1, device_id=partner, device_id_type=pl.DeviceIdType.MESH
        )
    pl.semaphore_wait(barrier, len(partners))

    sent = {None: [], 0: [], 1: []}

    def describe(phase, k, source, target):
        return pltpu.make_async_remote_copy(
            src_ref=source,
            dst_ref=target,
            send_sem=send_sems.at[phase, k],
            recv_sem=recv_sems.at[phase, k],
            device_id=target_of[k],
            device_id_type=pl.DeviceIdType.MESH,
        )

    def send(phase, k, source, target, when=None):
        describe(phase, k, source, target).start()
        sent[when].append((phase, k, source.shape))

    def await_arrival(phase, k, target):
        describe(phase, k, target, target).wait_recv()

    def by_parity(action):
        for p in range(2):
            pl.when(parity == p)(functools.partial(action, p))

    total = 2 * count
    anchor = 2 * g - 2

    def position(value):
        return lax.rem(value - anchor + total, total)

    def hit(at, w):
        return jnp.maximum(1 - jnp.abs(at - w), 0).astype(F32)

    def picked(pieces, weights):
        total_of = pieces[0] * weights[0]
        for piece, weight in zip(pieces[1:], weights[1:]):
            total_of = total_of + piece * weight
        return total_of

    def rows(w, size=1):
        return slice(w * block, (w + size) * block)

    def pair_rows(t):
        if isinstance(t, int):
            return rows(2 * t, 2)
        return pl.ds(pl.multiple_of(t * 2 * block, 2 * block), 2 * block)

    t_far, t_sib = 2 * parity, 2 - 2 * parity

    sib_from, far_from = 1 - parity, parity
    sib_to, far_to = 11 * parity, 11 * (1 - parity)
    send(0, FAR, dens_ref.at[pl.ds(far_from, 5)], full_win.at[pl.ds(far_to, 5), mine])
    send(0, FAR_CROSS, dens_ref.at[pl.ds(far_from, 5)], full_win.at[pl.ds(far_to, 5), mine])
    send(0, ORB, dens_ref, full_win.at[pl.ds(5, 6), mine])
    send(0, SIB, dens_ref.at[pl.ds(sib_from, 5)], full_win.at[pl.ds(sib_to, 5), mine])
    full_win[5:11, mine] = dens_ref[...]

    batch_hits = []
    for w in range(WIN):
        batch_hits.append([hit(position(batch_ref[0, j]), w) for j in range(WIN)])
    domain_hits = []
    for d in range(domains):
        places = [position(domain_ref[d, j]) for j in range(listed)]
        domain_hits.append([[hit(at, w) for at in places] for w in range(WIN)])
    masks = [[sum(hits[1:], hits[0]) for hits in by_window] for by_window in domain_hits]

    def sort_basis(w):
        values = picked(
            [basis_ref[:, j * block : (j + 1) * block] for j in range(WIN)], batch_hits[w]
        )
        high, low = split(values.T)
        basis_high[rows(w), :] = high
        basis_low[rows(w), :] = low
        basis_twice[rows(w), :] = high.astype(F32) + 2.0 * low.astype(F32)

    def sort_coefficients():
        for d in range(domains):
            for w in range(WIN):
                coef_now[rows(w), d * block : (d + 1) * block] = picked(
                    [coef_ref[d, j] for j in range(listed)], domain_hits[d][w]
                )

    fetch.wait()
    for w in range(WIN):
        sort_basis(w)

    def set_pair(t, value):
        pair_high[t], pair_low[t] = split(value)

    def set_cross(t, value):
        cross_high[t], cross_low[t] = split(value)

    def joined(aa, ab, ba, bb):
        return jnp.concatenate(
            [jnp.concatenate([aa, ab], axis=1), jnp.concatenate([ba, bb], axis=1)], axis=0
        )

    def full_pair(t):
        value = joined(*(full_win[6 * t + s] for s in range(4)))
        set_pair(t, 0.5 * (value + value.T))

    def full_cross(t):
        upper, lower = FULL_CROSS[t]
        set_cross(t, full_win[upper].T + full_win[lower])

    def window_pair(win, t):
        off = win[4 * t + 2]
        set_pair(t, joined(win[4 * t], off, off.T, win[4 * t + 1]))

    tile = 2 * block

    def over_points(step):
        def at_tile(i, carry):
            step(pl.ds(pl.multiple_of(i * tile, tile), tile))
            return carry

        lax.fori_loop(0, points // tile, at_tile, 0)

    def rho_pair(t, lanes):
        high = basis_high[pair_rows(t), lanes]
        image = mul(pair_high[t], high) + mul(pair_low[t], high)
        return jnp.sum(image * basis_twice[pair_rows(t), lanes], axis=0, keepdims=True)

    def rho_cross(t, lanes):
        source, sink = rows(2 * t + 1), rows(2 * t + 2)
        image = mul3(
            (cross_high[t], cross_low[t]), (basis_high[source, lanes], basis_low[source, lanes])
        )
        values = basis_high[sink, lanes].astype(F32) + basis_low[sink, lanes].astype(F32)
        return jnp.sum(image * values, axis=0, keepdims=True)

    def rho_own(lanes):
        rho_ref[:, lanes] = rho_pair(1, lanes) + rho_cross(1, lanes)

    def rho_sib(lanes):
        rho_ref[:, lanes] = rho_ref[:, lanes] + rho_pair(t_sib, lanes)

    def rho_far(lanes, crosses=(0,)):
        rho = rho_ref[:, lanes] + rho_pair(t_far, lanes)
        for t in crosses:
            rho = rho + rho_cross(t, lanes)
        potential = ext_ref[:, lanes] - jnp.exp(jnp.log(rho * rho + 1.0) * (1.0 / 6.0))
        scale = quad_ref[:, lanes] * potential
        for t in range(3):
            high, low = split(basis_twice[pair_rows(t), lanes] * scale)
            scaled_high[pair_rows(t), lanes] = high
            scaled_low[pair_rows(t), lanes] = low

    def fock_part(left, right):
        return mul_nt(basis_high[left, :], scaled_high[right, :]) + mul_nt(
            basis_high[left, :], scaled_low[right, :]
        )

    def put_pair(part, t, value):
        part[4 * t] = value[:block, :block]
        part[4 * t + 1] = value[block:, block:]
        part[4 * t + 2] = value[:block, block:]

    def fock_pair(part, t):
        value = fock_part(pair_rows(t), pair_rows(t))
        put_pair(part, t, 0.5 * (value + value.T))

    def fock_cross(part, t):
        low, high = rows(2 * t + 1), rows(2 * t + 2)
        part[4 * t + 3] = 0.5 * (fock_part(low, high) + fock_part(high, low).T)

    def outer(left, right):
        return mul3(
            (coef_high[left, :], coef_low[left, :]), (coef_high[right, :], coef_low[right, :]), mul_nt
        )

    def outer_pair(part, t):
        put_pair(part, t, outer(pair_rows(t), pair_rows(t)))

    def outer_cross(part, t):
        part[4 * t + 3] = outer(rows(2 * t + 1), rows(2 * t + 2))

    def gathered(phase, win, groups, on_own, on_sib, on_far):
        await_arrival(phase, ORB, win.at[groups["own"], theirs])
        groups["relay"](phase, win)
        on_own()
        groups["sib"](phase, win)
        on_sib()
        groups["far"](phase, win)
        on_far()

    BEFORE, OWN, AFTER = pl.ds(0, 4), pl.ds(4, 4), pl.ds(8, 3)
    group_of_sib = (AFTER, BEFORE)
    group_of_far = (BEFORE, AFTER)
    size_for_sib = (4, 3)
    size_for_far = (3, 4)

    def relay(phase, win):
        by_parity(lambda p: send(
            phase, RELAY,
            win.at[pl.ds(4, size_for_sib[p]), theirs],
            win.at[group_of_sib[1 - p], theirs], p,
        ))

    def sib_arrival(phase, win):
        def action(p):
            await_arrival(phase, SIB, win.at[group_of_sib[p], mine])
            await_arrival(phase, RELAY, win.at[group_of_sib[p], theirs])
        by_parity(action)

    def far_arrival(phase, win):
        def action(p):
            await_arrival(phase, FAR, win.at[group_of_far[p], mine])
            await_arrival(phase, FAR_CROSS, win.at[group_of_far[p], theirs])
        by_parity(action)

    unique_groups = dict(own=OWN, relay=relay, sib=sib_arrival, far=far_arrival)

    def full_relay(phase, win):
        send(
            phase, RELAY,
            win.at[pl.ds(5 + sib_from, 5), theirs], win.at[pl.ds(sib_to, 5), theirs],
        )

    def full_sib_arrival(phase, win):
        await_arrival(phase, SIB, win.at[pl.ds(11 * (1 - parity), 5), mine])
        await_arrival(phase, RELAY, win.at[pl.ds(11 * (1 - parity), 5), theirs])

    def full_far_arrival(phase, win):
        await_arrival(phase, FAR, win.at[pl.ds(11 * parity, 5), mine])
        await_arrival(phase, FAR_CROSS, win.at[pl.ds(11 * parity, 5), theirs])

    full_groups = dict(
        own=pl.ds(5, 6), relay=full_relay, sib=full_sib_arrival, far=full_far_arrival
    )

    def reduce_and_gather(index, make_pair, make_cross, meanwhile, on_own, on_sib, on_far):
        part, own, win = parts.at[index], owns.at[index], wins.at[index]
        far_recv, sib_recv, orb_recv = far_recvs.at[index], sib_recvs.at[index], orb_recvs.at[index]
        phase = 1 + 2 * index
        make_pair(part, t_far)
        make_cross(part, 0)

        def to_far(p):
            at = group_of_far[p]
            send(phase, FAR, part.at[at, mine], far_recv.at[0, pl.ds(0, at.size)], p)
            send(phase, FAR_CROSS, part.at[at, theirs], far_recv.at[1, pl.ds(0, at.size)], p)

        by_parity(to_far)
        make_pair(part, t_sib)

        def to_sib(p):
            at = group_of_sib[p]
            send(phase, SIB, part.at[at], sib_recv.at[pl.ds(0, at.size)], p)

        by_parity(to_sib)
        make_pair(part, 1)
        make_cross(part, 1)
        by_parity(lambda p: await_arrival(phase, SIB, sib_recv.at[pl.ds(0, size_for_sib[p])]))
        part[4:8] = part[4:8] + sib_recv[...]
        send(phase, ORB, part.at[pl.ds(4, 4), theirs], orb_recv)
        meanwhile()
        await_arrival(phase, ORB, orb_recv)

        def from_far(p):
            for k in range(2):
                await_arrival(phase, FAR + k, far_recv.at[k, pl.ds(0, size_for_far[p])])

        by_parity(from_far)
        own[...] = (part[4:8, mine] + orb_recv[...]) + (far_recv[0] + far_recv[1])

        def give(p):
            for k in range(2):
                send(
                    phase + 1, FAR + k,
                    own.at[pl.ds(0, size_for_far[p])], win.at[group_of_far[1 - p], mine], p,
                )

        by_parity(give)
        send(phase + 1, ORB, own, win.at[OWN, mine])
        by_parity(lambda p: send(
            phase + 1, SIB, own.at[pl.ds(0, size_for_sib[p])], win.at[group_of_sib[1 - p], mine], p
        ))
        win[4:8, mine] = own[...]
        gathered(phase + 1, win, unique_groups, *(functools.partial(f, win) for f in (on_own, on_sib, on_far)))

    def grad_pair(win, t):
        window_pair(win, t)
        at = pair_rows(t)
        grad_now[at, :] = grad_now[at, :] + mul3(
            (pair_high[t], pair_low[t]), (coef_high[at, :], coef_low[at, :])
        )

    def grad_cross(win, t):
        low, high = rows(2 * t + 1), rows(2 * t + 2)
        value = win[4 * t + 3]
        grad_now[low, :] = grad_now[low, :] + mul3(
            split(value), (coef_high[high, :], coef_low[high, :])
        )
        grad_now[high, :] = grad_now[high, :] + mul3(
            split(value.T), (coef_high[low, :], coef_low[low, :])
        )

    def split_coefficients():
        coef_high[...], coef_low[...] = split(coef_now[...])
        grad_now[...] = jnp.zeros_like(grad_now)

    def grad_own(win):
        grad_pair(win, 1)
        grad_cross(win, 1)

    def grad_sib(win):
        grad_pair(win, t_sib)

    def grad_far(win):
        grad_pair(win, t_far)
        grad_cross(win, 0)
        for d in range(domains):
            lanes = slice(d * block, (d + 1) * block)
            for w in range(WIN):
                grad_now[rows(w), lanes] = grad_now[rows(w), lanes] * masks[d][w]
            grad = grad_now[:, lanes]
            own = coef_now[:, lanes]
            overlap = mul3(split(own.T), split(grad))
            back = mul3((coef_high[:, lanes], coef_low[:, lanes]), split(overlap))
            coef_now[:, lanes] = own - STEP_SCALE * (grad - back)

    def density_own(win):
        window_pair(win, 1)
        set_cross(1, 2.0 * win[7].T)
        over_points(rho_own)

    def density_sib(win):
        window_pair(win, t_sib)
        over_points(rho_sib)

    def density_far(win):
        window_pair(win, t_far)
        set_cross(0, 2.0 * win[3].T)
        over_points(rho_far)

    def rho_first(lanes):
        rho_ref[:, lanes] = rho_pair(1, lanes)

    def first_own():
        full_pair(1)
        over_points(rho_first)

    def first_sib():
        full_pair(t_sib)
        over_points(rho_sib)

    def first_far():
        full_pair(t_far)
        full_cross(0)
        full_cross(1)
        over_points(functools.partial(rho_far, crosses=(0, 1)))

    def nothing():
        pass

    gathered(0, full_win, full_groups, first_own, first_sib, first_far)
    for iteration in range(ITERS):

        def before_gradient():
            if iteration == 0:
                sort_coefficients()
                split_coefficients()
            else:
                grad_now[...] = jnp.zeros_like(grad_now)

        reduce_and_gather(
            2 * iteration, fock_pair, fock_cross, before_gradient, grad_own, grad_sib, grad_far
        )
        coef_high[...], coef_low[...] = split(coef_now[...])
        if iteration + 1 < ITERS:
            reduce_and_gather(
                2 * iteration + 1, outer_pair, outer_cross, nothing,
                density_own, density_sib, density_far,
            )

    def put_full_pair(t):
        value = outer(pair_rows(t), pair_rows(t))
        full_part[6 * t] = value[:block, :block]
        full_part[6 * t + 1] = value[:block, block:]
        full_part[6 * t + 2] = value[block:, :block]
        full_part[6 * t + 3] = value[block:, block:]

    def put_full_cross(t):
        upper, lower = FULL_CROSS[t]
        value = outer(rows(2 * t + 1), rows(2 * t + 2))
        full_part[upper] = value
        full_part[lower] = value.T

    phase = send_sems.shape[0] - 1
    at_far, at_sib = pl.ds(11 * parity, 5), pl.ds(11 * (1 - parity), 5)
    put_full_pair(t_far)
    put_full_cross(0)
    put_full_cross(1)
    send(phase, FAR, full_part.at[at_far, mine], full_far.at[0])
    send(phase, FAR_CROSS, full_part.at[at_far, theirs], full_far.at[1])
    put_full_pair(t_sib)
    send(phase, SIB, full_part.at[at_sib], full_sib)
    put_full_pair(1)
    await_arrival(phase, SIB, full_sib)
    joint = pl.ds(5 + sib_from, 5)
    full_part[joint] = full_part[joint] + full_sib[...]
    send(phase, ORB, full_part.at[pl.ds(5, 6), theirs], full_orb)
    for d in range(domains):
        for j in range(listed):
            coef_out[d, j] = picked(
                [coef_now[rows(w), d * block : (d + 1) * block] for w in range(WIN)],
                [domain_hits[d][w][j] for w in range(WIN)],
            )
    await_arrival(phase, ORB, full_orb)
    dens_out[...] = full_part[5:11, mine] + full_orb[...]
    await_arrival(phase, FAR, full_far.at[0])
    await_arrival(phase, FAR_CROSS, full_far.at[1])
    joint = pl.ds(far_from, 5)
    dens_out[joint] = dens_out[joint] + (full_far[0] + full_far[1])

    def finish(p):
        for phase, k, (size, height, _) in sent[p]:
            amount = parts.at[0, pl.ds(0, size), pl.ds(0, height)]
            describe(phase, k, amount, amount).wait_send()

    finish(None)
    by_parity(finish)


def shards(
    density, basis_values, quad_weights, ext_potential, batch_blocks, domain_blocks, coefficients
):
    own_blocks, offsets, half, block = density.shape
    points, width = basis_values.shape[1:]
    domains, listed = coefficients.shape[:2]
    sums = 2 * ITERS - 1
    vmem = pl.BlockSpec(memory_space=pltpu.VMEM)
    smem = pl.BlockSpec(memory_space=pltpu.SMEM)
    dens, coef = pl.pallas_call(
        functools.partial(kernel, lax.axis_size("grid")),
        out_shape=(
            jax.ShapeDtypeStruct((own_blocks * offsets, half, block), F32),
            jax.ShapeDtypeStruct(coefficients.shape, F32),
        ),
        in_specs=[vmem, pl.BlockSpec(memory_space=pl.ANY), vmem, vmem, smem, smem, vmem],
        out_specs=(vmem, vmem),
        scratch_shapes=[
            pltpu.VMEM((points, width), F32),
            pltpu.VMEM((width, points), BF16),
            pltpu.VMEM((width, points), BF16),
            pltpu.VMEM((width, points), F32),
            pltpu.VMEM((width, points), BF16),
            pltpu.VMEM((width, points), BF16),
            pltpu.VMEM((1, points), F32),
            pltpu.VMEM((3, 2 * block, 2 * block), BF16),
            pltpu.VMEM((3, 2 * block, 2 * block), BF16),
            pltpu.VMEM((2, block, block), BF16),
            pltpu.VMEM((2, block, block), BF16),
            pltpu.VMEM((width, domains * block), F32),
            pltpu.VMEM((width, domains * block), BF16),
            pltpu.VMEM((width, domains * block), BF16),
            pltpu.VMEM((width, domains * block), F32),
            pltpu.VMEM((16, block, block), F32),
            pltpu.VMEM((16, block, block), F32),
            pltpu.VMEM((2, 5, half, block), F32),
            pltpu.VMEM((5, block, block), F32),
            pltpu.VMEM((6, half, block), F32),
            pltpu.VMEM((sums, 11, block, block), F32),
            pltpu.VMEM((sums, 2, 4, half, block), F32),
            pltpu.VMEM((sums, 4, block, block), F32),
            pltpu.VMEM((sums, 4, half, block), F32),
            pltpu.VMEM((sums, 4, half, block), F32),
            pltpu.VMEM((sums, 11, block, block), F32),
            pltpu.SemaphoreType.DMA,
            pltpu.SemaphoreType.DMA((2 * sums + 2, 5)),
            pltpu.SemaphoreType.DMA((2 * sums + 2, 5)),
        ],
        compiler_params=pltpu.CompilerParams(collective_id=0, has_side_effects=True),
    )(
        density.reshape(own_blocks * offsets, half, block),
        basis_values[0],
        quad_weights,
        ext_potential,
        batch_blocks,
        domain_blocks,
        coefficients,
    )
    return dens.reshape(density.shape), coef


def solution(mesh):
    in_specs = (
        P("grid", None, "orb", None),
        P(("grid", "orb"), None, None),
        P(("grid", "orb"), None),
        P(("grid", "orb"), None),
        P(("grid", "orb"), None),
        P(("grid", "orb"), None),
        P(("grid", "orb"), None, None, None),
    )
    out_specs = (P("grid", None, "orb", None), P(("grid", "orb"), None, None, None))
    return jax.shard_map(shards, mesh=mesh, in_specs=in_specs, out_specs=out_specs, check_vma=False)
```

time: 108 us -> 98.1 us (0.908)
  the two profiles are of different devices: /device:TPU:33 before, /device:TPU:2 now
where the time goes in v1:
time: 98.1 us; the launch traced here: 97.9 us
  Pallas kernels  93.8 us (96%)
  local copies, waits for them, and re-layouts  3.49 us (4%)
    pallas_call x1, Pallas kernels, shards(): pl.pallas_call(functools.partial(kernel, lax.axis_size('grid')), out_shap...  93.8 us
    unnamed x2, local copies, waits for them, and re-layouts  3.49 us

profile of v1, /device:TPU:2, one launch (start us, length us, event | category | flops | bytes accessed | tf_op | source)
XLA Modules:
  0.0 97.9 jit_solution(9445155978938195643)
XLA Ops:
  0.6 93.8 %shard_map.86 = (f32[6,64,128]{2,1,0:T(8,128)}, f32[2,4,128,128]{3,2,1,0:T(8,128)}) custom-call(f32[6,64,128]{2,1,0:T(8,128)} %bitcast.4, f32[1280,768]{1,0:T(8,128)} %bitcast.3, f32[1,1280]{1,0:T(1,128)} %quad_ref.1, f32[1,1280]{1,0:T(1,128)} %ext_ref.1, s32[1,6]{1,0:T(1,128)} %batch_ref.1, s32[2,4]{1,0:T(2,128)} %domain_ref.1, f32[2,4,128,128]{3,2,1,0:T(8,128)} %coef_ref.1), custom_call_target="tpu_custom_call" | custom-call | tf_op jit(solution)/shard_map/pallas_call | solution.py:511
  94.4 1.6 %copy.11 = f32[2,3,64,128]{3,2,1,0:T(8,128)} copy(f32[2,3,64,128]{3,2,1,0:T(8,128)} %bitcast.5) | data formatting | bytes 393216
  96.0 1.9 %copy.12 = f32[2,4,128,128]{3,2,1,0:T(8,128)} copy(f32[2,4,128,128]{3,2,1,0:T(8,128)} %get-tuple-element.9) | data formatting | bytes 1048576
